TPU v7x, 32 devices: a whole 2x2x4 slice. The times are simulated.
32 devices in a mesh: shot: 8 (over z, y), rcv: 4 (over x, core).
Axes of the slice: x: 2, y: 2, z: 4, core: 2. Of those that a mesh axis runs over, the one named last changes fastest.
Arguments:
- data_matrix: bfloat16 [2, 16, 1024, 1024], P(None, None, 'shot', 'rcv'), may hold values from -12 to 12
- shot_records: bfloat16 [2, 16, 1024, 1024], P(None, None, 'rcv', 'shot'), may hold values from -4 to 4
- live: int32 [1024, 1024], P('rcv', 'shot'), may hold values 0 or 1
Outputs:
- predicted: bfloat16 [2, 16, 1024, 1024], P(None, None, 'rcv', 'shot')
- primaries: bfloat16 [2, 16, 1024, 1024], P(None, None, 'rcv', 'shot')
All inputs are finite; a program needn't handle non-finite values. No bound on the sum of `live` on one device may be relied on, other than what follows from the above.
Results may differ from a plain program's by a relative error of at most 0.013.
Values may be sent and summed in bfloat16 or wider, within the bound.
A program may use at most 128 MiB of HBM per device.

v0:
```python
import jax
import jax.numpy as jnp
from jax import lax
from jax.sharding import PartitionSpec as P


def complex_product(left, right):
    prod = jnp.einsum("afrk,bfks->abfrs", left, right, preferred_element_type=jnp.float32)
    return jnp.stack((prod[0, 0] - prod[1, 1], prod[0, 1] + prod[1, 0]))


def shards(data_matrix, shot_records, live):
    records = shot_records * live.astype(jnp.bfloat16)[None, None]
    own_rows = records.shape[2]
    partial_terms = complex_product(
        lax.all_gather(data_matrix, "shot", axis=2, tiled=True), records
    )
    summed = lax.psum(partial_terms.astype(jnp.bfloat16), "rcv").astype(jnp.float32)
    total = lax.dynamic_slice_in_dim(summed, lax.axis_index("rcv") * own_rows, own_rows, 2)
    rec = records.astype(jnp.float32)
    num_re = jnp.sum(total[0] * rec[0] + total[1] * rec[1], axis=1)
    num_im = jnp.sum(total[0] * rec[1] - total[1] * rec[0], axis=1)
    power = jnp.sum(total[0] * total[0] + total[1] * total[1], axis=1)
    sum_re, sum_im, sum_power = lax.psum((num_re, num_im, power), "rcv")
    points = float(own_rows * lax.axis_size("rcv"))
    power_mean = sum_power / points + 1e-06
    filt_re = (sum_re / points / power_mean)[:, None, :]
    filt_im = (sum_im / points / power_mean)[:, None, :]
    out_re = rec[0] - (filt_re * total[0] - filt_im * total[1])
    out_im = rec[1] - (filt_re * total[1] + filt_im * total[0])
    primaries = jnp.stack((out_re, out_im)).astype(jnp.bfloat16)
    return (total.astype(jnp.bfloat16), primaries)


def solution(mesh):
    in_specs = (P(None, None, "shot", "rcv"), P(None, None, "rcv", "shot"), P("rcv", "shot"))
    out_specs = (P(None, None, "rcv", "shot"), P(None, None, "rcv", "shot"))
    return jax.shard_map(shards, mesh=mesh, in_specs=in_specs, out_specs=out_specs, check_vma=False)
```

profile of v0, /device:TPU:0, one launch (start us, length us, event | category | flops | bytes accessed | tf_op | source)
XLA Modules:
  0.0 466.1 jit_solution(6643771911731964899)
XLA Ops:
  7.2 0.0 all-gather.2.cloned.1.call-start
  7.2 3.1 copy.7
  10.3 0.0 all-gather.2.cloned.1.call-update
  10.4 0.0 copy-start.1
  10.4 0.0 all-reduce.3.cloned.1.call-start
  10.4 1.5 copy-done
  11.9 2.6 copy.6
  14.5 0.0 copy-done.1
  14.5 0.1 copy.5
  14.6 4.0 multiply_convert_fusion
  18.7 222.4 %all-gather.2.cloned.1.call-done = bf16[2,16,1024,256]{3,2,0,1:T(8,128)(2,1)} async-done(((bf16[2,16,128,256]{3,2,0,1:T(8,128)(2,1)}), bf16[2,16,1024,256]{3,2,0,1:T(8,128)(2,1)}) %all-gather.2.cloned.1.call-update) | async-done | bytes 16777232 | tf_op jit(solution)/shard_map/all_gather | solution.py:16
  241.1 17.6 %fusion.2 = f32[2,2,16,1024,128]{3,4,0,1,2:T(8,128)} fusion(bf16[2,16,1024,256]{3,2,0,1:T(8,128)(2,1)} %all-gather.2.cloned.1.call-done, bf16[2,16,256,128,1]{2,3,1,0,4:T(8,128)(2,1)S(1)} %get-tuple-element.15), kind=kOutput, calls=%fused_computation.2 | convolution fusion | flops 4294967296 | bytes 52428800 | tf_op jit(solution)/shard_map/afrk,bfks->abfrs/dot_general | solution.py:8
  258.7 6.6 %fusion.9 = bf16[1,16,1024,128]{2,3,1,0:T(8,128)(2,1)S(1)} fusion(f32[2,2,16,1024,128]{3,4,0,1,2:T(8,128)} %fusion.2), kind=kLoop, calls=%fused_computation.11 | loop fusion | flops 4194304 | bytes 20971520 | tf_op jit(solution)/shard_map/add | solution.py:9
  265.3 8.8 %fusion.8 = bf16[1,16,1024,128]{2,3,1,0:T(8,128)(2,1)} fusion(f32[2,2,16,1024,128]{3,4,0,1,2:T(8,128)} %fusion.2), kind=kLoop, calls=%fused_computation.10 | loop fusion | flops 4194304 | bytes 20971520 | tf_op jit(solution)/shard_map/sub | solution.py:9
  274.0 6.2 %pad_maximum_fusion = bf16[2,16,1024,128]{2,3,1,0:T(8,128)(2,1)} fusion(bf16[1,16,1024,128]{2,3,1,0:T(8,128)(2,1)S(1)} %fusion.9, bf16[1,16,1024,128]{2,3,1,0:T(8,128)(2,1)} %fusion.8), kind=kLoop, calls=%fused_computation.9 | loop fusion | flops 4194304 | bytes 16777216 | tf_op jit(solution)/shard_map/stack | solution.py:9
  280.2 0.0 all-reduce.3.cloned.1.call-update
  280.2 151.2 %all-reduce.3.cloned.1.call-done = bf16[2,16,1024,128]{2,3,1,0:T(8,128)(2,1)} async-done(((bf16[2,16,1024,128]{2,3,1,0:T(8,128)(2,1)}), bf16[2,16,1024,128]{2,3,1,0:T(8,128)(2,1)}) %all-reduce.3.cloned.1.call-update) | async-done | bytes 8388624 | tf_op jit(solution)/shard_map/psum | solution.py:18
  431.4 4.1 dynamic-slice_convert_fusion
  435.5 2.4 copy.11
  437.9 4.6 add_reduce_fusion.1
  442.5 10.3 %all-reduce = (f32[16,128]{1,0:T(8,128)S(1)}, f32[16,128]{1,0:T(8,128)S(1)}, f32[16,128]{1,0:T(8,128)S(1)}) all-reduce(f32[16,128]{1,0:T(8,128)S(1)} %get-tuple-element.5, f32[16,128]{1,0:T(8,128)S(1)} %get-tuple-element.6, f32[16,128]{1,0:T(8,128)S(1)} %get-tuple-element.4), channel_id=1, replica_groups=mesh['shot'=8,'rcv'=4] {'rcv'}, use_global_device_ids=true, to_apply=%region_6.0 | all-reduce | flops 6144 | bytes 49152 | tf_op jit(solution)/shard_map/psum | solution.py:24
  452.8 3.8 subtract_convert_fusion.1
  456.7 0.2 pad_maximum_fusion.1
  456.9 2.4 copy.12
  (3 shorter events, 0.0 us)
Async XLA Ops:
  7.2 233.9 %all-gather.2.cloned.1.call-start = ((), (), s32[]{:S(2)}) async-start(), calls=%async_computation | async-start | bytes 18874368 | tf_op jit(solution)/shard_map/all_gather | solution.py:16
  10.3 1.6 copy-start
  10.4 4.1 copy-start.1
  10.4 421.0 %all-reduce.3.cloned.1.call-start = ((), (), s32[]{:S(2)}) async-start(), calls=%async_computation.1 | async-start | bytes 16777216 | tf_op jit(solution)/shard_map/psum | solution.py:18
Sparse Core Ops, SparseCore 0:
  10.8 230.2 all-gather.1
  280.4 151.0 all-reduce.2
where the time goes:
time: 466 us
  waiting for transfers between devices  374 us (80%)
  other arithmetic  38.4 us (8%)
  matrix products  17.6 us (4%)
  between operations  14.1 us (3%)
  local copies, waits for them, and re-layouts  12.1 us (3%)
  blocking collectives  10.3 us (2%)
    all_gather x1, waiting for transfers between devices, shards(): lax.all_gather(data_matrix, 'shot', axis=2, tiled=True)  222 us
    psum x1, waiting for transfers between devices, shards(): lax.psum(partial_terms.astype(jnp.bfloat16), 'rcv').astype(jnp.float32)  151 us
    dot_general x1, matrix products, complex_product(): jnp.einsum('afrk,bfks->abfrs', left, right, preferred_element_type=jnp.fl...  17.6 us
    unnamed x8, local copies, waits for them, and re-layouts  12 us
    psum x1, blocking collectives, shards(): sum_re, sum_im, sum_power = lax.psum((num_re, num_im, power), 'rcv')  10.3 us
  transfers between devices with their start and end apart: 2, of which 2 were waited for; matrix products, arithmetic and copies ran while one was open for 1% of the time, Pallas kernels for 0%

commit v1 on v0

--- a/solution.py
+++ b/solution.py
@@ -2,6 +2,27 @@
 import jax.numpy as jnp
 from jax import lax
 from jax.sharding import PartitionSpec as P
+
+
+def gather_around(x, axis, dim):
+    peers, place, width = (lax.axis_size(axis), lax.axis_index(axis), x.shape[dim])
+    ahead = [(i, (i + 1) % peers) for i in range(peers)]
+    downward = [(i, (i - 1) % peers) for i in range(peers)]
+    out = jnp.zeros((*x.shape[:dim], peers * width, *x.shape[dim + 1 :]), x.dtype)
+    out = lax.dynamic_update_slice_in_dim(out, x, place * width, axis=dim)
+    from_left = from_right = x
+    middle = peers // 2
+    for step in range(1, middle + 1):
+        from_left = lax.ppermute(from_left, axis, ahead)
+        out = lax.dynamic_update_slice_in_dim(
+            out, from_left, (place - step) % peers * width, axis=dim
+        )
+        if step < peers - middle:
+            from_right = lax.ppermute(from_right, axis, downward)
+            out = lax.dynamic_update_slice_in_dim(
+                out, from_right, (place + step) % peers * width, axis=dim
+            )
+    return out
 
 
 def complex_product(left, right):
@@ -12,9 +33,7 @@
 def shards(data_matrix, shot_records, live):
     records = shot_records * live.astype(jnp.bfloat16)[None, None]
     own_rows = records.shape[2]
-    partial_terms = complex_product(
-        lax.all_gather(data_matrix, "shot", axis=2, tiled=True), records
-    )
+    partial_terms = complex_product(gather_around(data_matrix, "shot", 2), records)
     summed = lax.psum(partial_terms.astype(jnp.bfloat16), "rcv").astype(jnp.float32)
     total = lax.dynamic_slice_in_dim(summed, lax.axis_index("rcv") * own_rows, own_rows, 2)
     rec = records.astype(jnp.float32)

time: 466 us -> 562 us (1.21)
  waiting for transfers between devices: 374 us -> 423 us
  local copies, waits for them, and re-layouts: 12.1 us -> 37.4 us
  starting transfers between devices: 0.08 us -> 19.7 us
    ppermute x0 -> x7, waiting for transfers between devices: none -> 271 us  [the longest x4 271 us: gather_around(): from_left = lax.ppermute(from_left, axis, ahead)]
    all_gather x1 -> x0, waiting for transfers between devices: 222 us -> none  [shards(): lax.all_gather(data_matrix, 'shot', axis=2, tiled=True)]
    dynamic_update_slice x0 -> x8, local copies, waits for them, and re-layouts: none -> 21.5 us  [the longest x4 12.5 us: gather_around(): lax.dynamic_update_slice_in_dim(out, from_left, (place - step) % peers *...]
    ppermute x0 -> x7, starting transfers between devices: none -> 19.7 us  [the longest x4 10.5 us: gather_around(): from_left = lax.ppermute(from_left, axis, ahead)]
    broadcast_in_dim x0 -> x1, local copies, waits for them, and re-layouts: none -> 5.84 us  [gather_around(): jnp.zeros((*x.shape[:dim], peers * width, *x.shape[dim + 1:]), x.dtype)]
    unnamed x8 -> x11, local copies, waits for them, and re-layouts: 12 us -> 10 us
  transfers between devices with their start and end apart: 2 -> 8, of which waited for: 2 -> 5; matrix products, arithmetic and copies ran while one was open for 1% -> 6% of each run, Pallas kernels for 0% -> 0%
where the time goes in v1:
time: 562 us; the launch traced here: 561 us
  waiting for transfers between devices  423 us (75%)
  other arithmetic  39.3 us (7%)
  local copies, waits for them, and re-layouts  37.4 us (7%)
  starting transfers between devices  19.7 us (4%)
  matrix products  17.6 us (3%)
  between operations  14.1 us (3%)
  blocking collectives  10.3 us (2%)
    ppermute x4, waiting for transfers between devices, gather_around(): from_left = lax.ppermute(from_left, axis, ahead)  271 us
    psum x1, waiting for transfers between devices, shards(): lax.psum(partial_terms.astype(jnp.bfloat16), 'rcv').astype(jnp.float32)  151 us
    dot_general x1, matrix products, complex_product(): jnp.einsum('afrk,bfks->abfrs', left, right, preferred_element_type=jnp.fl...  17.6 us
    dynamic_update_slice x4, local copies, waits for them, and re-layouts, gather_around(): lax.dynamic_update_slice_in_dim(out, from_left, (place - step) % peers *...  12.5 us
  transfers between devices with their start and end apart: 8, of which 5 were waited for; matrix products, arithmetic and copies ran while one was open for 6% of the time, Pallas kernels for 0%

profile of v1, /device:TPU:0, one launch (start us, length us, event | category | flops | bytes accessed | tf_op | source)
XLA Modules:
  0.0 561.3 jit_solution(9740877775313810079)
XLA Ops:
  10.2 3.1 collective-permute-start.1
  13.3 87.0 %collective-permute-done = bf16[2,16,128,256]{3,2,1,0:T(8,128)(2,1)S(1)} collective-permute-done((bf16[2,16,128,256]{3,2,1,0:T(8,128)(2,1)}, bf16[2,16,128,256]{3,2,1,0:T(8,128)(2,1)S(1)}, u32[]{:S(2)}, u32[]{:S(2)}) %collective-permute-start) | collective-permute-done | bytes 2097184 | tf_op jit(solution)/shard_map/ppermute | solution.py:16
  104.1 3.1 collective-permute-start.3
  107.2 85.9 %collective-permute-done.2 = bf16[2,16,128,256]{3,2,1,0:T(8,128)(2,1)} collective-permute-done((bf16[2,16,128,256]{3,2,1,0:T(8,128)(2,1)S(1)}, bf16[2,16,128,256]{3,2,1,0:T(8,128)(2,1)}, u32[]{:S(2)}, u32[]{:S(2)}) %collective-permute-start.2) | collective-permute-done | bytes 2097184 | tf_op jit(solution)/shard_map/ppermute | solution.py:16
  196.6 3.9 copy.6
  203.6 4.0 multiply_convert_fusion
  207.7 76.9 %collective-permute-done.4 = bf16[2,16,128,256]{3,2,1,0:T(8,128)(2,1)} collective-permute-done((bf16[2,16,128,256]{3,2,1,0:T(8,128)(2,1)}, bf16[2,16,128,256]{3,2,1,0:T(8,128)(2,1)}, u32[]{:S(2)}, u32[]{:S(2)}) %collective-permute-start.4) | collective-permute-done | bytes 2097184 | tf_op jit(solution)/shard_map/ppermute | solution.py:16
  287.1 5.8 %broadcast_in_dim.2 = bf16[2,16,1024,256]{3,2,0,1:T(8,128)(2,1)} broadcast(bf16[]{:T(256)} %constant.59.clone.1), dimensions={} | broadcast | bytes 16777218 | tf_op jit(solution)/shard_map/broadcast_in_dim | solution.py:11
  294.3 3.2 copy_dynamic-update-slice_fusion.6
  298.9 3.1 copy_dynamic-update-slice_fusion.4
  302.0 3.1 copy_dynamic-update-slice_fusion.3
  305.1 3.1 copy_dynamic-update-slice_fusion.2
  308.2 3.1 copy_dynamic-update-slice_fusion.1
  311.3 21.6 %collective-permute-done.6 = bf16[2,16,128,256]{3,2,1,0:T(8,128)(2,1)} collective-permute-done((bf16[2,16,128,256]{3,2,1,0:T(8,128)(2,1)}, bf16[2,16,128,256]{3,2,1,0:T(8,128)(2,1)}, u32[]{:S(2)}, u32[]{:S(2)}) %collective-permute-start.6) | collective-permute-done | bytes 2097184 | tf_op jit(solution)/shard_map/ppermute | solution.py:16
  332.9 3.1 copy_dynamic-update-slice_fusion
  336.0 17.6 %fusion.2 = f32[2,2,16,1024,128]{3,4,0,1,2:T(8,128)} fusion(bf16[2,16,1024,256]{3,2,0,1:T(8,128)(2,1)} %copy_dynamic-update-slice_fusion, bf16[2,16,256,128,1]{2,3,1,0,4:T(8,128)(2,1)S(1)} %get-tuple-element.15), kind=kOutput, calls=%fused_computation.2 | convolution fusion | flops 4294967296 | bytes 52428800 | tf_op jit(solution)/shard_map/afrk,bfks->abfrs/dot_general | solution.py:29
  353.6 6.6 %fusion.9 = bf16[1,16,1024,128]{2,3,1,0:T(8,128)(2,1)S(1)} fusion(f32[2,2,16,1024,128]{3,4,0,1,2:T(8,128)} %fusion.2), kind=kLoop, calls=%fused_computation.11 | loop fusion | flops 4194304 | bytes 20971520 | tf_op jit(solution)/shard_map/add | solution.py:30
  360.2 8.8 %fusion.8 = bf16[1,16,1024,128]{2,3,1,0:T(8,128)(2,1)} fusion(f32[2,2,16,1024,128]{3,4,0,1,2:T(8,128)} %fusion.2), kind=kLoop, calls=%fused_computation.10 | loop fusion | flops 4194304 | bytes 20971520 | tf_op jit(solution)/shard_map/sub | solution.py:30
  368.9 6.2 %pad_maximum_fusion = bf16[2,16,1024,128]{2,3,1,0:T(8,128)(2,1)} fusion(bf16[1,16,1024,128]{2,3,1,0:T(8,128)(2,1)S(1)} %fusion.9, bf16[1,16,1024,128]{2,3,1,0:T(8,128)(2,1)} %fusion.8), kind=kLoop, calls=%fused_computation.9 | loop fusion | flops 4194304 | bytes 16777216 | tf_op jit(solution)/shard_map/stack | solution.py:30
  375.1 151.5 %all-reduce.3.cloned.1.call-done = bf16[2,16,1024,128]{2,3,1,0:T(8,128)(2,1)} async-done(((bf16[2,16,1024,128]{2,3,1,0:T(8,128)(2,1)}), bf16[2,16,1024,128]{2,3,1,0:T(8,128)(2,1)}) %all-reduce.3.cloned.1.call-update) | async-done | bytes 8388624 | tf_op jit(solution)/shard_map/psum | solution.py:37
  526.6 4.1 dynamic-slice_convert_fusion
  533.1 4.6 add_reduce_fusion.1
  537.7 10.3 %all-reduce = (f32[16,128]{1,0:T(8,128)S(1)}, f32[16,128]{1,0:T(8,128)S(1)}, f32[16,128]{1,0:T(8,128)S(1)}) all-reduce(f32[16,128]{1,0:T(8,128)S(1)} %get-tuple-element.5, f32[16,128]{1,0:T(8,128)S(1)} %get-tuple-element.6, f32[16,128]{1,0:T(8,128)S(1)} %get-tuple-element.4), channel_id=1, replica_groups=mesh['shot'=8,'rcv'=4] {'rcv'}, use_global_device_ids=true, to_apply=%region_6.7 | all-reduce | flops 6144 | bytes 49152 | tf_op jit(solution)/shard_map/psum | solution.py:43
  548.0 3.8 subtract_convert_fusion.1
  (26 shorter events, 23.7 us)
Async XLA Ops:
  7.2 519.5 %all-reduce.3.cloned.1.call-start = ((), (), s32[]{:S(2)}) async-start(), calls=%async_computation | async-start | bytes 16777216 | tf_op jit(solution)/shard_map/psum | solution.py:37
  7.2 93.2 %collective-permute-start = (bf16[2,16,128,256]{3,2,1,0:T(8,128)(2,1)}, bf16[2,16,128,256]{3,2,1,0:T(8,128)(2,1)S(1)}, u32[]{:S(2)}, u32[]{:S(2)}) collective-permute-start(bf16[2,16,128,256]{3,2,1,0:T(8,128)(2,1)} %param.3), channel_id=1, source_target_pairs={{0,4},{4,8},{8,12},{12,16},{16,20},{20,24},{24,28},{28,0},{1,5},{5... | collective-permute-start | bytes 6291464 | tf_op jit(solution)/shard_map/ppermute | solution.py:16
  10.2 93.8 %collective-permute-start.1 = (bf16[2,16,128,256]{3,2,1,0:T(8,128)(2,1)}, bf16[2,16,128,256]{3,2,1,0:T(8,128)(2,1)S(1)}, u32[]{:S(2)}, u32[]{:S(2)}) collective-permute-start(bf16[2,16,128,256]{3,2,1,0:T(8,128)(2,1)} %param.3), channel_id=1, source_target_pairs={{0,28},{4,0},{8,4},{12,8},{16,12},{20,16},{24,20},{28,24},{1,29},{... | collective-permute-start | bytes 6291464 | tf_op jit(solution)/shard_map/ppermute | solution.py:21
  100.4 1.3 copy-start.1
  101.7 91.3 %collective-permute-start.2 = (bf16[2,16,128,256]{3,2,1,0:T(8,128)(2,1)S(1)}, bf16[2,16,128,256]{3,2,1,0:T(8,128)(2,1)}, u32[]{:S(2)}, u32[]{:S(2)}) collective-permute-start(bf16[2,16,128,256]{3,2,1,0:T(8,128)(2,1)S(1)} %collective-permute-done), channel_id=1, source_target_pairs={{0,4},{4,8},{8,12},{12,16},{16,20},{20,24},{24,28},{28,0},{1,5},{5... | collective-permute-start | bytes 6291464 | tf_op jit(solution)/shard_map/ppermute | solution.py:16
  104.1 96.5 %copy-start.2 = (bf16[2,16,128,256]{3,2,1,0:T(8,128)(2,1)}, bf16[2,16,128,256]{3,2,1,0:T(8,128)(2,1)S(1)}, u32[]{:S(2)}) copy-start(bf16[2,16,128,256]{3,2,1,0:T(8,128)(2,1)S(1)} %collective-permute-done.1) | copy-start | bytes 6291460
  104.1 96.5 %collective-permute-start.3 = (bf16[2,16,128,256]{3,2,1,0:T(8,128)(2,1)S(1)}, bf16[2,16,128,256]{3,2,1,0:T(8,128)(2,1)}, u32[]{:S(2)}, u32[]{:S(2)}) collective-permute-start(bf16[2,16,128,256]{3,2,1,0:T(8,128)(2,1)S(1)} %collective-permute-done.1), channel_id=1, source_target_pairs={{0,28},{4,0},{8,4},{12,8},{16,12},{20,16},{24,20},{28,24},{1,29},{... | collective-permute-start | bytes 6291464 | tf_op jit(solution)/shard_map/ppermute | solution.py:21
  193.0 91.6 %collective-permute-start.4 = (bf16[2,16,128,256]{3,2,1,0:T(8,128)(2,1)}, bf16[2,16,128,256]{3,2,1,0:T(8,128)(2,1)}, u32[]{:S(2)}, u32[]{:S(2)}) collective-permute-start(bf16[2,16,128,256]{3,2,1,0:T(8,128)(2,1)} %collective-permute-done.2), channel_id=1, source_target_pairs={{0,4},{4,8},{8,12},{12,16},{16,20},{20,24},{24,28},{28,0},{1,5},{5... | collective-permute-start | bytes 6291464 | tf_op jit(solution)/shard_map/ppermute | solution.py:16
  200.6 107.6 %collective-permute-start.5 = (bf16[2,16,128,256]{3,2,1,0:T(8,128)(2,1)}, bf16[2,16,128,256]{3,2,1,0:T(8,128)(2,1)}, u32[]{:S(2)}, u32[]{:S(2)}) collective-permute-start(bf16[2,16,128,256]{3,2,1,0:T(8,128)(2,1)} %collective-permute-done.3), channel_id=1, source_target_pairs={{0,28},{4,0},{8,4},{12,8},{16,12},{20,16},{24,20},{28,24},{1,29},{... | collective-permute-start | bytes 6291464 | tf_op jit(solution)/shard_map/ppermute | solution.py:21
  207.7 85.2 %copy-start = (bf16[2,16,128,256]{3,2,1,0:T(8,128)(2,1)S(1)}, bf16[2,16,128,256]{3,2,1,0:T(8,128)(2,1)}, u32[]{:S(2)}) copy-start(bf16[2,16,128,256]{3,2,1,0:T(8,128)(2,1)} %param.3) | copy-start | bytes 6291460
  284.6 48.3 %collective-permute-start.6 = (bf16[2,16,128,256]{3,2,1,0:T(8,128)(2,1)}, bf16[2,16,128,256]{3,2,1,0:T(8,128)(2,1)}, u32[]{:S(2)}, u32[]{:S(2)}) collective-permute-start(bf16[2,16,128,256]{3,2,1,0:T(8,128)(2,1)} %collective-permute-done.4), channel_id=1, source_target_pairs={{0,4},{4,8},{8,12},{12,16},{16,20},{20,24},{24,28},{28,0},{1,5},{5... | collective-permute-start | bytes 6291464 | tf_op jit(solution)/shard_map/ppermute | solution.py:16
  294.3 3.2 copy-start.3
Sparse Core Ops, SparseCore 0:
  375.3 151.3 all-reduce.2
